TPU v7x, 128 devices: a whole 4x4x4 slice. The times are simulated.
128 devices in a mesh: mem: 2 (over core), state: 64 (over y, x, z).
Axes of the slice: x: 4, y: 4, z: 4, core: 2. Of those that a mesh axis runs over, the one named last changes fastest.
Arguments:
- background_ensemble: bfloat16 [80, 4194304], P('mem', 'state'), may hold values from -6 to 6
- measured_segment_index: int32 [2, 256], replicated, may hold values from 0 to 127
- measured_place_within_segment: int32 [2, 256], replicated, may hold values from 0 to 32767
- measured_readings: float32 [2, 256], replicated, may hold values from -6 to 6
- measured_noise_spread: float32 [2, 256], replicated, may hold values from 0.25 to 4
- measured_damping_weight: float32 [2, 256], replicated, may hold values from 0.3 to 1
- measured_cutoff_extent: int32 [2, 256], replicated, may hold values from 1 to 1024
Outputs:
- analysis: bfloat16 [80, 4194304], P('mem', 'state')
Inputs may be any that keep to these rules, and one draw needn't show every extreme that they name: measured_segment_index numbers the blocks of 32768 state values in the order of the state dimension. measured_place_within_segment is a position inside the owner's block.
All inputs are finite; a program needn't handle non-finite values.
Results may differ from a plain program's by a relative error of at most 0.0051.
Values may be sent and summed in bfloat16 or wider, within the bound.
No kernel may reach another device: no remote copies, remote signals or barrier semaphores. Data moves between devices by JAX's collectives and lax.ppermute only.
A program may use at most 64 MiB of HBM per device.

v0:
```python
import jax
import jax.numpy as jnp
from jax import lax
from jax.sharding import Mesh
from jax.sharding import PartitionSpec as P

ENSEMBLE_COUNT = 80
SD = 32768
B = 2
LB = 128
BLK = 4096
STATE = ("state_0", "state_1", "state_2")


def split_up(array, dim, size):
    dims = array.shape
    blocks = array.reshape(*dims[:dim], size, dims[dim] // size, *dims[dim + 1 :])
    return jnp.moveaxis(blocks, dim, 0)


def sum_at_owner(array, axis, dim):
    blocks = split_up(array, dim, lax.axis_size(axis))
    arrived = lax.all_to_all(blocks, axis, split_axis=0, concat_axis=0, tiled=True)
    return arrived.sum(axis=0)


def summed_rows(array, axes, dim):
    far, near = axes
    own = sum_at_owner(split_up(array, dim, lax.axis_size(far)), near, dim + 1)
    return jnp.sum(lax.all_to_all(own, far, 0, 0, tiled=True), axis=0)


def filled_up(lines, size):
    spare = -lines.shape[0] % size
    if not spare:
        return lines
    return jnp.concatenate([lines, jnp.zeros((spare, *lines.shape[1:]), lines.dtype)])


def sent_to_all(array, axis):
    size = lax.axis_size(axis)
    return lax.all_to_all(
        jnp.broadcast_to(array[None], (size, *array.shape)), axis, 0, 0, tiled=True
    )


def joined_along(blocks, dim):
    blocks = jnp.moveaxis(blocks, 0, dim)
    dims = blocks.shape
    return blocks.reshape(*dims[:dim], dims[dim] * dims[dim + 1], *dims[dim + 2 :])


def gather_axes(array, axes, dim):
    far, near = axes
    blocks = sent_to_all(sent_to_all(array, far), near)
    return joined_along(blocks.swapaxes(0, 1).reshape(-1, *array.shape), dim)


def total_of(array, axes):
    lines = array.reshape(-1)
    own = summed_rows(filled_up(lines, lax.axis_size(axes[0]) * lax.axis_size(axes[1])), axes, 0)
    whole = gather_axes(own, axes, 0)
    return whole[: len(lines)].reshape(array.shape)


def observe_stats(prior_ens, values, variances):
    centre = jnp.mean(prior_ens, axis=0)
    anomaly = prior_ens - centre
    prior_var = jnp.sum(anomaly * anomaly, axis=0) / (ENSEMBLE_COUNT - 1) + 1e-06
    post_var = 1.0 / (1.0 / prior_var + 1.0 / variances)
    post_mean = post_var * (centre / prior_var + values / variances)
    shrink = jnp.sqrt(post_var / prior_var)
    increment = (post_mean - centre + (shrink - 1.0) * anomaly).astype(jnp.bfloat16)
    scaling = 1.0 / ((ENSEMBLE_COUNT - 1) * prior_var)
    return (increment, anomaly.astype(jnp.bfloat16), scaling)


def taper_weights(columns, obs_index, taper_row, reach_row):
    distance = jnp.abs(columns[:, None] // LB - obs_index[None, :] // LB).astype(jnp.float32)
    return taper_row[None, :] * jnp.maximum(
        0.0, 1.0 - distance / (reach_row[None, :].astype(jnp.float32) + 1.0)
    )


def update_block(
    block_values, columns, obs_index, taper_row, reach_row, increment, anomaly, scaling
):
    values = block_values.astype(jnp.float32)
    centred = (values - jnp.mean(values, axis=0)).astype(jnp.bfloat16)
    covariance = lax.dot_general(
        centred, anomaly, (((0,), (0,)), ((), ())), preferred_element_type=jnp.float32
    )
    gain_matrix = (
        taper_weights(columns, obs_index, taper_row, reach_row) * covariance * scaling[None, :]
    ).astype(jnp.bfloat16)
    change = lax.dot_general(
        increment, gain_matrix, (((1,), (1,)), ((), ())), preferred_element_type=jnp.float32
    )
    return (values + change).astype(jnp.bfloat16)


def collect_prior(realization_vectors, owner_row, local_row, my_block, col_offset):
    picked = jnp.take(realization_vectors, col_offset + local_row, axis=1).astype(jnp.float32)
    return jnp.where((owner_row == my_block)[None, :], picked, 0.0)


def apply_batch(
    realization_vectors, column_base, obs_index, taper_row, reach_row, increment, anomaly, scaling
):

    def advance(block_no, buffer):
        start_col = block_no * BLK
        block_values = lax.dynamic_slice_in_dim(buffer, start_col, BLK, 1)
        columns = column_base + start_col + jnp.arange(BLK, dtype=jnp.int32)
        renewed = update_block(
            block_values, columns, obs_index, taper_row, reach_row, increment, anomaly, scaling
        )
        return lax.dynamic_update_slice_in_dim(buffer, renewed, start_col, 1)

    return lax.fori_loop(0, realization_vectors.shape[1] // BLK, advance, realization_vectors)


def on_device(
    background_ensemble,
    measured_segment_index,
    measured_place_within_segment,
    measured_readings,
    measured_noise_spread,
    measured_damping_weight,
    measured_cutoff_extent,
):
    pieces = lax.axis_size("mem")
    member_row = lax.axis_index("mem")
    slab_index = lax.axis_index(STATE)
    my_block = slab_index * pieces + member_row
    realization_vectors = lax.all_to_all(
        background_ensemble, "mem", split_axis=1, concat_axis=0, tiled=True
    )
    column_base = my_block * SD
    col_offset = 0
    for batch_no in range(B):
        if batch_no == 0:
            prior_ens = total_of(
                collect_prior(
                    realization_vectors,
                    measured_segment_index[0],
                    measured_place_within_segment[0],
                    my_block,
                    col_offset,
                ),
                ("mem", ("state_0", "state_1", "state_2")),
            )
        else:
            prior_ens = total_of(
                collect_prior(
                    realization_vectors,
                    measured_segment_index[batch_no],
                    measured_place_within_segment[batch_no],
                    my_block,
                    col_offset,
                ),
                ("mem", ("state_0", "state_1", "state_2")),
            )
        obs_index = measured_segment_index[batch_no] * SD + measured_place_within_segment[batch_no]
        increment, anomaly, scaling = observe_stats(
            prior_ens, measured_readings[batch_no], measured_noise_spread[batch_no]
        )
        realization_vectors = apply_batch(
            realization_vectors,
            column_base,
            obs_index,
            measured_damping_weight[batch_no],
            measured_cutoff_extent[batch_no],
            increment,
            anomaly,
            scaling,
        )
    return lax.all_to_all(realization_vectors, "mem", split_axis=0, concat_axis=1, tiled=True)


def solution(mesh):
    torus = Mesh(
        mesh.devices.reshape(mesh.shape["mem"], 4, 4, 4), ("mem", "state_0", "state_1", "state_2")
    )
    in_specs = (P("mem", STATE), P(), P(), P(), P(), P(), P())
    out_specs = P("mem", STATE)
    return jax.shard_map(
        on_device, mesh=torus, in_specs=in_specs, out_specs=out_specs, check_vma=False
    )
```

profile of v0, /device:TPU:1, one launch (start us, length us, event | category | flops | bytes accessed | tf_op | source)
XLA Modules:
  0.0 211.1 jit_solution(6932354710521923166)
XLA Ops:
  0.0 5.2 %copy.47 = bf16[5,2,8,32768]{3,2,0,1:T(8,128)(2,1)} copy(bf16[5,2,8,32768]{3,2,1,0:T(8,128)(2,1)} %bitcast.89) | data formatting | bytes 10485760 | tf_op jit(solution)/shard_map/all_to_all | solution.py:136
  5.2 7.5 %all-to-all-start = ((bf16[40,2,32768]{2,0,1:T(8,128)(2,1)}), bf16[40,2,32768]{2,0,1:T(8,128)(2,1)}, u32[]{:S(2)}, u32[]{:S(2)}) async-start(bf16[40,2,32768]{2,0,1:T(8,128)(2,1)} %bitcast.87), calls=%async_computation | async-start | bytes 10485760 | tf_op jit(solution)/shard_map/all_to_all | solution.py:136
  12.8 4.8 %all-to-all-done = bf16[40,2,32768]{2,0,1:T(8,128)(2,1)} async-done(((bf16[40,2,32768]{2,0,1:T(8,128)(2,1)}), bf16[40,2,32768]{2,0,1:T(8,128)(2,1)}, u32[]{:S(2)}, u32[]{:S(2)}) %all-to-all-start) | async-done | bytes 5242912 | tf_op jit(solution)/shard_map/all_to_all | solution.py:136
  17.6 9.5 %copy.31 = bf16[80,32768]{0,1:T(8,128)(2,1)} copy(bf16[80,32768]{1,0:T(8,128)(2,1)} %bitcast.9) | data formatting | bytes 10485760 | tf_op jit(solution)/shard_map/all_to_all | solution.py:136
  27.2 5.2 %gather_fusion = bf16[256,80]{1,0:T(8,128)(2,1)S(1)} fusion(bf16[80,32768]{0,1:T(8,128)(2,1)} %copy.31, s32[1024]{0:T(1024)S(1)} %pad_clamp_fusion.1), kind=kCustom, calls=%fused_computation.clone | custom fusion | bytes 82944 | tf_op jit(solution)/shard_map/jit(_take)/gather | solution.py:103
  33.4 11.2 %all-to-all-start.1 = ((f32[64,2,160]{2,1,0:T(2,128)}), f32[64,2,160]{2,1,0:T(2,128)S(1)}, u32[]{:S(2)}, u32[]{:S(2)}) async-start(f32[64,2,160]{2,1,0:T(2,128)} %copy.33), calls=%async_computation.1 | async-start | bytes 262144 | tf_op jit(solution)/shard_map/all_to_all | solution.py:23
  44.7 8.7 %all-to-all-done.1 = f32[64,2,160]{2,1,0:T(2,128)S(1)} async-done(((f32[64,2,160]{2,1,0:T(2,128)}), f32[64,2,160]{2,1,0:T(2,128)S(1)}, u32[]{:S(2)}, u32[]{:S(2)}) %all-to-all-start.1) | async-done | bytes 81952 | tf_op jit(solution)/shard_map/all_to_all | solution.py:23
  53.5 5.2 %all_to_all.88 = f32[2,1,160]{2,1,0:T(1,128)S(1)} all-to-all(f32[2,1,160]{2,1,0:T(1,128)S(1)} %all_to_all.65), channel_id=1, replica_groups=mesh['mem'=2,'state_0'=4,'state_1'=4,'state_2'=4] {'mem'}, dimensions={0} | all-to-all | bytes 2560 | tf_op jit(solution)/shard_map/all_to_all | solution.py:30
  58.7 3.7 %all_to_all.89 = f32[2,1,160]{2,1,0:T(1,128)S(1)} all-to-all(f32[2,1,160]{2,1,0:T(1,128)S(1)} %broadcast_in_dim.94), channel_id=1, replica_groups=mesh['mem'=2,'state_0'=4,'state_1'=4,'state_2'=4] {'mem'}, dimensions={0} | all-to-all | bytes 2560 | tf_op jit(solution)/shard_map/all_to_all | solution.py:42
  63.1 4.7 %all-to-all-start.4 = ((f32[64,2,160]{2,1,0:T(2,128)}), f32[64,2,160]{2,1,0:T(2,128)S(1)}, u32[]{:S(2)}, u32[]{:S(2)}) async-start(f32[64,2,160]{2,1,0:T(2,128)} %broadcast_in_dim.96), calls=%async_computation.4 | async-start | bytes 262144 | tf_op jit(solution)/shard_map/all_to_all | solution.py:42
  67.8 8.7 %all-to-all-done.4 = f32[64,2,160]{2,1,0:T(2,128)S(1)} async-done(((f32[64,2,160]{2,1,0:T(2,128)}), f32[64,2,160]{2,1,0:T(2,128)S(1)}, u32[]{:S(2)}, u32[]{:S(2)}) %all-to-all-start.4) | async-done | bytes 81952 | tf_op jit(solution)/shard_map/all_to_all | solution.py:42
  76.9 33.8 %while.32 = (s32[]{:T(128)}, bf16[80,32768]{1,0:T(8,128)(2,1)}, f32[1,256]{1,0:T(1,128)S(1)}, s32[]{:T(128)}, s32[1,256]{1,0:T(1,128)S(1)}, /*index=5*/s32[256]{...) while((s32[]{:T(128)}, bf16[80,32768]{1,0:T(8,128)(2,1)}, ...), condition=%wide.region_6.8_spmd, body=%wide.region_4.7_spmd.sunk | while | flops 348720640 | bytes 3467987 | solution.py:120
  76.9 1.2 convert_reduce_fusion.4
  78.2 2.9 %fusion.48 = bf16[80,32768]{1,0:T(8,128)(2,1)} fusion(bf16[80,32768]{1,0:T(8,128)(2,1)} %get-tuple-element.801, s32[]{:T(128)S(6)} %select_n.138, bf16[80,256]{1,0:T(8,128)(2,1)S(1)} %get-tuple-element.825, bf16[80,4096]{1,0:T(8,128)(2,1)S(1)} %get-tuple-element.770, bf16[80,256]{1,0:T(8,128)(2,1)S(1)} %get-tuple-element.823, ...), kind=kOutput, calls=%fused_computation.8.clone.1 | convolution fusion | flops 347996160 | bytes 2084868 | tf_op jit(solution)/shard_map/while/body/eval_jaxpr/dot_general | solution.py:96
  81.1 1.2 convert_reduce_fusion.4
  82.4 2.9 %fusion.48 = bf16[80,32768]{1,0:T(8,128)(2,1)} fusion(bf16[80,32768]{1,0:T(8,128)(2,1)} %get-tuple-element.801, s32[]{:T(128)S(6)} %select_n.138, bf16[80,256]{1,0:T(8,128)(2,1)S(1)} %get-tuple-element.825, bf16[80,4096]{1,0:T(8,128)(2,1)S(1)} %get-tuple-element.770, bf16[80,256]{1,0:T(8,128)(2,1)S(1)} %get-tuple-element.823, ...), kind=kOutput, calls=%fused_computation.8.clone.1 | convolution fusion | flops 347996160 | bytes 2084868 | tf_op jit(solution)/shard_map/while/body/eval_jaxpr/dot_general | solution.py:96
  86.6 2.9 %fusion.48 = bf16[80,32768]{1,0:T(8,128)(2,1)} fusion(bf16[80,32768]{1,0:T(8,128)(2,1)} %get-tuple-element.801, s32[]{:T(128)S(6)} %select_n.138, bf16[80,256]{1,0:T(8,128)(2,1)S(1)} %get-tuple-element.825, bf16[80,4096]{1,0:T(8,128)(2,1)S(1)} %get-tuple-element.770, bf16[80,256]{1,0:T(8,128)(2,1)S(1)} %get-tuple-element.823, ...), kind=kOutput, calls=%fused_computation.8.clone.1 | convolution fusion | flops 347996160 | bytes 2084868 | tf_op jit(solution)/shard_map/while/body/eval_jaxpr/dot_general | solution.py:96
  89.6 1.2 convert_reduce_fusion.4
  90.9 2.9 %fusion.48 = bf16[80,32768]{1,0:T(8,128)(2,1)} fusion(bf16[80,32768]{1,0:T(8,128)(2,1)} %get-tuple-element.801, s32[]{:T(128)S(6)} %select_n.138, bf16[80,256]{1,0:T(8,128)(2,1)S(1)} %get-tuple-element.825, bf16[80,4096]{1,0:T(8,128)(2,1)S(1)} %get-tuple-element.770, bf16[80,256]{1,0:T(8,128)(2,1)S(1)} %get-tuple-element.823, ...), kind=kOutput, calls=%fused_computation.8.clone.1 | convolution fusion | flops 347996160 | bytes 2084868 | tf_op jit(solution)/shard_map/while/body/eval_jaxpr/dot_general | solution.py:96
  95.1 2.9 %fusion.48 = bf16[80,32768]{1,0:T(8,128)(2,1)} fusion(bf16[80,32768]{1,0:T(8,128)(2,1)} %get-tuple-element.801, s32[]{:T(128)S(6)} %select_n.138, bf16[80,256]{1,0:T(8,128)(2,1)S(1)} %get-tuple-element.825, bf16[80,4096]{1,0:T(8,128)(2,1)S(1)} %get-tuple-element.770, bf16[80,256]{1,0:T(8,128)(2,1)S(1)} %get-tuple-element.823, ...), kind=kOutput, calls=%fused_computation.8.clone.1 | convolution fusion | flops 347996160 | bytes 2084868 | tf_op jit(solution)/shard_map/while/body/eval_jaxpr/dot_general | solution.py:96
  98.0 1.2 convert_reduce_fusion.4
  99.3 2.9 %fusion.48 = bf16[80,32768]{1,0:T(8,128)(2,1)} fusion(bf16[80,32768]{1,0:T(8,128)(2,1)} %get-tuple-element.801, s32[]{:T(128)S(6)} %select_n.138, bf16[80,256]{1,0:T(8,128)(2,1)S(1)} %get-tuple-element.825, bf16[80,4096]{1,0:T(8,128)(2,1)S(1)} %get-tuple-element.770, bf16[80,256]{1,0:T(8,128)(2,1)S(1)} %get-tuple-element.823, ...), kind=kOutput, calls=%fused_computation.8.clone.1 | convolution fusion | flops 347996160 | bytes 2084868 | tf_op jit(solution)/shard_map/while/body/eval_jaxpr/dot_general | solution.py:96
  102.2 1.2 convert_reduce_fusion.4
  103.5 2.9 %fusion.48 = bf16[80,32768]{1,0:T(8,128)(2,1)} fusion(bf16[80,32768]{1,0:T(8,128)(2,1)} %get-tuple-element.801, s32[]{:T(128)S(6)} %select_n.138, bf16[80,256]{1,0:T(8,128)(2,1)S(1)} %get-tuple-element.825, bf16[80,4096]{1,0:T(8,128)(2,1)S(1)} %get-tuple-element.770, bf16[80,256]{1,0:T(8,128)(2,1)S(1)} %get-tuple-element.823, ...), kind=kOutput, calls=%fused_computation.8.clone.1 | convolution fusion | flops 347996160 | bytes 2084868 | tf_op jit(solution)/shard_map/while/body/eval_jaxpr/dot_general | solution.py:96
  106.4 1.2 convert_reduce_fusion.4
  107.7 2.9 %fusion.48 = bf16[80,32768]{1,0:T(8,128)(2,1)} fusion(bf16[80,32768]{1,0:T(8,128)(2,1)} %get-tuple-element.801, s32[]{:T(128)S(6)} %select_n.138, bf16[80,256]{1,0:T(8,128)(2,1)S(1)} %get-tuple-element.825, bf16[80,4096]{1,0:T(8,128)(2,1)S(1)} %get-tuple-element.770, bf16[80,256]{1,0:T(8,128)(2,1)S(1)} %get-tuple-element.823, ...), kind=kOutput, calls=%fused_computation.8.clone.1 | convolution fusion | flops 347996160 | bytes 2084868 | tf_op jit(solution)/shard_map/while/body/eval_jaxpr/dot_general | solution.py:96
  110.6 9.5 %copy.35 = bf16[80,32768]{0,1:T(8,128)(2,1)} copy(bf16[80,32768]{1,0:T(8,128)(2,1)} %get-tuple-element.831) | data formatting | bytes 10485760 | tf_op jit(solution)/shard_map/while | solution.py:120
  120.1 5.2 %gather_fusion.1 = bf16[256,80]{1,0:T(8,128)(2,1)S(1)} fusion(bf16[80,32768]{0,1:T(8,128)(2,1)} %copy.35, s32[1024]{0:T(1024)S(1)} %pad_clamp_fusion), kind=kCustom, calls=%fused_computation.1.clone | custom fusion | bytes 82944 | tf_op jit(solution)/shard_map/jit(_take)/gather | solution.py:103
  125.8 13.5 %all_to_all.90 = f32[64,2,160]{2,1,0:T(2,128)S(1)} all-to-all(f32[64,2,160]{2,1,0:T(2,128)S(1)} %copy.37), channel_id=1, replica_groups=mesh['mem'=2,'state_0'=4,'state_1'=4,'state_2'=4] {'state_0','state_1','..., dimensions={0} | all-to-all | bytes 163840 | tf_op jit(solution)/shard_map/all_to_all | solution.py:23
  139.4 6.2 %all_to_all.91 = f32[2,1,160]{2,1,0:T(1,128)S(1)} all-to-all(f32[2,1,160]{2,1,0:T(1,128)S(1)} %all_to_all.70), channel_id=1, replica_groups=mesh['mem'=2,'state_0'=4,'state_1'=4,'state_2'=4] {'mem'}, dimensions={0} | all-to-all | bytes 2560 | tf_op jit(solution)/shard_map/all_to_all | solution.py:30
  145.7 3.7 %all_to_all.92 = f32[2,1,160]{2,1,0:T(1,128)S(1)} all-to-all(f32[2,1,160]{2,1,0:T(1,128)S(1)} %broadcast_in_dim.99), channel_id=1, replica_groups=mesh['mem'=2,'state_0'=4,'state_1'=4,'state_2'=4] {'mem'}, dimensions={0} | all-to-all | bytes 2560 | tf_op jit(solution)/shard_map/all_to_all | solution.py:42
  150.1 4.9 %all-to-all-start.8 = ((f32[64,2,160]{2,1,0:T(2,128)}), f32[64,2,160]{2,1,0:T(2,128)S(1)}, u32[]{:S(2)}, u32[]{:S(2)}) async-start(f32[64,2,160]{2,1,0:T(2,128)} %broadcast_in_dim.101), calls=%async_computation.8 | async-start | bytes 262144 | tf_op jit(solution)/shard_map/all_to_all | solution.py:42
  154.9 8.6 %all-to-all-done.8 = f32[64,2,160]{2,1,0:T(2,128)S(1)} async-done(((f32[64,2,160]{2,1,0:T(2,128)}), f32[64,2,160]{2,1,0:T(2,128)S(1)}, u32[]{:S(2)}, u32[]{:S(2)}) %all-to-all-start.8) | async-done | bytes 81952 | tf_op jit(solution)/shard_map/all_to_all | solution.py:42
  163.8 33.8 %while.33 = (s32[]{:T(128)}, bf16[80,32768]{1,0:T(8,128)(2,1)}, f32[1,256]{1,0:T(1,128)S(1)}, s32[]{:T(128)}, s32[1,256]{1,0:T(1,128)S(1)}, /*index=5*/s32[256]{...) while((s32[]{:T(128)}, bf16[80,32768]{1,0:T(8,128)(2,1)}, ...), condition=%wide.region_13.15_spmd, body=%wide.region_11.14_spmd.sunk | while | flops 348720640 | bytes 3467987 | solution.py:120
  163.8 1.2 convert_reduce_fusion.5
  165.1 2.9 %fusion.52 = bf16[80,32768]{1,0:T(8,128)(2,1)} fusion(bf16[80,32768]{1,0:T(8,128)(2,1)} %get-tuple-element.846, s32[]{:T(128)S(6)} %select_n.141, bf16[80,256]{1,0:T(8,128)(2,1)S(1)} %get-tuple-element.870, bf16[80,4096]{1,0:T(8,128)(2,1)S(1)} %get-tuple-element.783, bf16[80,256]{1,0:T(8,128)(2,1)S(1)} %get-tuple-element.868, ...), kind=kOutput, calls=%fused_computation.38.clone.1 | convolution fusion | flops 347996160 | bytes 2084868 | tf_op jit(solution)/shard_map/while/body/eval_jaxpr/dot_general | solution.py:96
  168.0 1.2 convert_reduce_fusion.5
  169.3 2.9 %fusion.52 = bf16[80,32768]{1,0:T(8,128)(2,1)} fusion(bf16[80,32768]{1,0:T(8,128)(2,1)} %get-tuple-element.846, s32[]{:T(128)S(6)} %select_n.141, bf16[80,256]{1,0:T(8,128)(2,1)S(1)} %get-tuple-element.870, bf16[80,4096]{1,0:T(8,128)(2,1)S(1)} %get-tuple-element.783, bf16[80,256]{1,0:T(8,128)(2,1)S(1)} %get-tuple-element.868, ...), kind=kOutput, calls=%fused_computation.38.clone.1 | convolution fusion | flops 347996160 | bytes 2084868 | tf_op jit(solution)/shard_map/while/body/eval_jaxpr/dot_general | solution.py:96
  172.3 1.2 convert_reduce_fusion.5
  173.6 2.9 %fusion.52 = bf16[80,32768]{1,0:T(8,128)(2,1)} fusion(bf16[80,32768]{1,0:T(8,128)(2,1)} %get-tuple-element.846, s32[]{:T(128)S(6)} %select_n.141, bf16[80,256]{1,0:T(8,128)(2,1)S(1)} %get-tuple-element.870, bf16[80,4096]{1,0:T(8,128)(2,1)S(1)} %get-tuple-element.783, bf16[80,256]{1,0:T(8,128)(2,1)S(1)} %get-tuple-element.868, ...), kind=kOutput, calls=%fused_computation.38.clone.1 | convolution fusion | flops 347996160 | bytes 2084868 | tf_op jit(solution)/shard_map/while/body/eval_jaxpr/dot_general | solution.py:96
  177.8 3.0 %fusion.52 = bf16[80,32768]{1,0:T(8,128)(2,1)} fusion(bf16[80,32768]{1,0:T(8,128)(2,1)} %get-tuple-element.846, s32[]{:T(128)S(6)} %select_n.141, bf16[80,256]{1,0:T(8,128)(2,1)S(1)} %get-tuple-element.870, bf16[80,4096]{1,0:T(8,128)(2,1)S(1)} %get-tuple-element.783, bf16[80,256]{1,0:T(8,128)(2,1)S(1)} %get-tuple-element.868, ...), kind=kOutput, calls=%fused_computation.38.clone.1 | convolution fusion | flops 347996160 | bytes 2084868 | tf_op jit(solution)/shard_map/while/body/eval_jaxpr/dot_general | solution.py:96
  180.7 1.2 convert_reduce_fusion.5
  182.0 2.9 %fusion.52 = bf16[80,32768]{1,0:T(8,128)(2,1)} fusion(bf16[80,32768]{1,0:T(8,128)(2,1)} %get-tuple-element.846, s32[]{:T(128)S(6)} %select_n.141, bf16[80,256]{1,0:T(8,128)(2,1)S(1)} %get-tuple-element.870, bf16[80,4096]{1,0:T(8,128)(2,1)S(1)} %get-tuple-element.783, bf16[80,256]{1,0:T(8,128)(2,1)S(1)} %get-tuple-element.868, ...), kind=kOutput, calls=%fused_computation.38.clone.1 | convolution fusion | flops 347996160 | bytes 2084868 | tf_op jit(solution)/shard_map/while/body/eval_jaxpr/dot_general | solution.py:96
  186.2 2.9 %fusion.52 = bf16[80,32768]{1,0:T(8,128)(2,1)} fusion(bf16[80,32768]{1,0:T(8,128)(2,1)} %get-tuple-element.846, s32[]{:T(128)S(6)} %select_n.141, bf16[80,256]{1,0:T(8,128)(2,1)S(1)} %get-tuple-element.870, bf16[80,4096]{1,0:T(8,128)(2,1)S(1)} %get-tuple-element.783, bf16[80,256]{1,0:T(8,128)(2,1)S(1)} %get-tuple-element.868, ...), kind=kOutput, calls=%fused_computation.38.clone.1 | convolution fusion | flops 347996160 | bytes 2084868 | tf_op jit(solution)/shard_map/while/body/eval_jaxpr/dot_general | solution.py:96
  190.4 2.9 %fusion.52 = bf16[80,32768]{1,0:T(8,128)(2,1)} fusion(bf16[80,32768]{1,0:T(8,128)(2,1)} %get-tuple-element.846, s32[]{:T(128)S(6)} %select_n.141, bf16[80,256]{1,0:T(8,128)(2,1)S(1)} %get-tuple-element.870, bf16[80,4096]{1,0:T(8,128)(2,1)S(1)} %get-tuple-element.783, bf16[80,256]{1,0:T(8,128)(2,1)S(1)} %get-tuple-element.868, ...), kind=kOutput, calls=%fused_computation.38.clone.1 | convolution fusion | flops 347996160 | bytes 2084868 | tf_op jit(solution)/shard_map/while/body/eval_jaxpr/dot_general | solution.py:96
  194.7 2.9 %fusion.52 = bf16[80,32768]{1,0:T(8,128)(2,1)} fusion(bf16[80,32768]{1,0:T(8,128)(2,1)} %get-tuple-element.846, s32[]{:T(128)S(6)} %select_n.141, bf16[80,256]{1,0:T(8,128)(2,1)S(1)} %get-tuple-element.870, bf16[80,4096]{1,0:T(8,128)(2,1)S(1)} %get-tuple-element.783, bf16[80,256]{1,0:T(8,128)(2,1)S(1)} %get-tuple-element.868, ...), kind=kOutput, calls=%fused_computation.38.clone.1 | convolution fusion | flops 347996160 | bytes 2084868 | tf_op jit(solution)/shard_map/while/body/eval_jaxpr/dot_general | solution.py:96
  197.6 10.8 %all_to_all.93 = bf16[2,40,32768]{2,1,0:T(8,128)(2,1)S(1)} all-to-all(bf16[2,40,32768]{2,1,0:T(8,128)(2,1)} %bitcast.29), channel_id=1, replica_groups=mesh['mem'=2,'state_0'=4,'state_1'=4,'state_2'=4] {'mem'}, dimensions={0} | all-to-all | bytes 10485760 | tf_op jit(solution)/shard_map/all_to_all | solution.py:178
  208.4 2.7 %copy.43 = bf16[2,5,8,32768]{3,2,0,1:T(8,128)(2,1)} copy(bf16[2,5,8,32768]{3,2,1,0:T(8,128)(2,1)S(1)} %bitcast.88) | data formatting | bytes 10485760 | tf_op jit(solution)/shard_map/all_to_all | solution.py:178
  (145 shorter events, 11.9 us)
Async XLA Ops:
  5.2 7.5 %copy-start = (s32[2,256]{1,0:T(2,128)S(1)}, s32[2,256]{1,0:T(2,128)}, u32[]{:S(2)}) copy-start(s32[2,256]{1,0:T(2,128)} %param.14) | copy-start | bytes 6148
  5.2 7.5 %copy-start.4 = (s32[2,256]{1,0:T(2,128)S(1)}, s32[2,256]{1,0:T(2,128)}, u32[]{:S(2)}) copy-start(s32[2,256]{1,0:T(2,128)} %param.19) | copy-start | bytes 6148
  5.2 7.5 %copy-start.5 = (s32[2,256]{1,0:T(2,128)S(1)}, s32[2,256]{1,0:T(2,128)}, u32[]{:S(2)}) copy-start(s32[2,256]{1,0:T(2,128)} %param.15) | copy-start | bytes 6148
  5.2 12.4 %all-to-all-start = ((bf16[40,2,32768]{2,0,1:T(8,128)(2,1)}), bf16[40,2,32768]{2,0,1:T(8,128)(2,1)}, u32[]{:S(2)}, u32[]{:S(2)}) async-start(bf16[40,2,32768]{2,0,1:T(8,128)(2,1)} %bitcast.87), calls=%async_computation | async-start | bytes 10485760 | tf_op jit(solution)/shard_map/all_to_all | solution.py:136
  17.6 27.1 %copy-start.1 = (f32[2,256]{1,0:T(2,128)S(1)}, f32[2,256]{1,0:T(2,128)}, u32[]{:S(2)}) copy-start(f32[2,256]{1,0:T(2,128)} %param.18) | copy-start | bytes 6148
  17.6 59.2 %copy-start.2 = (f32[2,256]{1,0:T(2,128)S(1)}, f32[2,256]{1,0:T(2,128)}, u32[]{:S(2)}) copy-start(f32[2,256]{1,0:T(2,128)} %param.16) | copy-start | bytes 6148
  17.6 59.2 %copy-start.3 = (f32[2,256]{1,0:T(2,128)S(1)}, f32[2,256]{1,0:T(2,128)}, u32[]{:S(2)}) copy-start(f32[2,256]{1,0:T(2,128)} %param.17) | copy-start | bytes 6148
  33.4 20.0 %all-to-all-start.1 = ((f32[64,2,160]{2,1,0:T(2,128)}), f32[64,2,160]{2,1,0:T(2,128)S(1)}, u32[]{:S(2)}, u32[]{:S(2)}) async-start(f32[64,2,160]{2,1,0:T(2,128)} %copy.33), calls=%async_computation.1 | async-start | bytes 262144 | tf_op jit(solution)/shard_map/all_to_all | solution.py:23
  63.1 13.4 %all-to-all-start.4 = ((f32[64,2,160]{2,1,0:T(2,128)}), f32[64,2,160]{2,1,0:T(2,128)S(1)}, u32[]{:S(2)}, u32[]{:S(2)}) async-start(f32[64,2,160]{2,1,0:T(2,128)} %broadcast_in_dim.96), calls=%async_computation.4 | async-start | bytes 262144 | tf_op jit(solution)/shard_map/all_to_all | solution.py:42
  150.1 13.4 %all-to-all-start.8 = ((f32[64,2,160]{2,1,0:T(2,128)}), f32[64,2,160]{2,1,0:T(2,128)S(1)}, u32[]{:S(2)}, u32[]{:S(2)}) async-start(f32[64,2,160]{2,1,0:T(2,128)} %broadcast_in_dim.101), calls=%async_computation.8 | async-start | bytes 262144 | tf_op jit(solution)/shard_map/all_to_all | solution.py:42
where the time goes:
time: 213 us; the launch traced here: 211 us
  matrix products  46.8 us (22%)
  blocking collectives  43.1 us (20%)
  local copies, waits for them, and re-layouts  40.2 us (19%)
  waiting for transfers between devices  30.8 us (14%)
  starting transfers between devices  28.3 us (13%)
  other arithmetic  21.1 us (10%)
    dot_general x16, matrix products, update_block(): lax.dot_general(increment, gain_matrix, (((1,), (1,)), ((), ())), preferr...  46.8 us
    reduce_sum x16, other arithmetic, update_block(): centred = (values - jnp.mean(values, axis=0)).astype(jnp.bfloat16)  19.4 us
    all_to_all x2, waiting for transfers between devices, sent_to_all(): lax.all_to_all(jnp.broadcast_to(array[None], (size, *array.shape)), axis,...  17.3 us
    all_to_all x2, local copies, waits for them, and re-layouts, on_device(): lax.all_to_all(background_ensemble, 'mem', split_axis=1, concat_axis=0, t...  14.7 us
    all_to_all x1, blocking collectives, sum_at_owner(): lax.all_to_all(blocks, axis, split_axis=0, concat_axis=0, tiled=True)  13.5 us
    all_to_all x2, blocking collectives, summed_rows(): return jnp.sum(lax.all_to_all(own, far, 0, 0, tiled=True), axis=0)  11.4 us
    all_to_all x1, starting transfers between devices, sum_at_owner(): lax.all_to_all(blocks, axis, split_axis=0, concat_axis=0, tiled=True)  11.2 us
    all_to_all x1, blocking collectives, on_device(): lax.all_to_all(realization_vectors, 'mem', split_axis=0, concat_axis=1, t...  10.8 us
  transfers between devices with their start and end apart: 4, of which 4 were waited for; matrix products, arithmetic and copies ran while one was open for 0% of the time, Pallas kernels for 0%

commit v1 on v0

--- a/solution.py
+++ b/solution.py
@@ -175,7 +175,12 @@
             anomaly,
             scaling,
         )
-    return lax.all_to_all(realization_vectors, "mem", split_axis=0, concat_axis=1, tiled=True)
+    return jnp.concatenate(
+        lax.all_to_all(
+            jnp.stack(jnp.split(realization_vectors, lax.axis_size("mem"), axis=0)), "mem", 0, 0
+        ),
+        axis=1,
+    )
 
 
 def solution(mesh):

time: 213 us -> 215 us (level)
  local copies, waits for them, and re-layouts: 40.2 us -> 43.1 us
    another operation x0 -> x1, local copies, waits for them, and re-layouts: none -> 2.87 us  [on_device(): jnp.stack(jnp.split(realization_vectors, lax.axis_size('mem'), axis=0))]
    all_to_all x1 -> x0, local copies, waits for them, and re-layouts: 2.73 us -> none  [on_device(): lax.all_to_all(realization_vectors, 'mem', split_axis=0, concat_axis=1, t...]
    reshape x0 -> x1, local copies, waits for them, and re-layouts: none -> 2.73 us  [on_device(): jnp.concatenate(lax.all_to_all(jnp.stack(jnp.split(realization_vectors, l...]
where the time goes in v1:
time: 215 us; the launch traced here: 213 us
  matrix products  46.8 us (22%)
  local copies, waits for them, and re-layouts  43.1 us (20%)
  blocking collectives  41.7 us (19%)
  waiting for transfers between devices  30.8 us (14%)
  starting transfers between devices  28.3 us (13%)
  other arithmetic  21.6 us (10%)
    dot_general x16, matrix products, update_block(): lax.dot_general(increment, gain_matrix, (((1,), (1,)), ((), ())), preferr...  46.8 us
    reduce_sum x16, other arithmetic, update_block(): centred = (values - jnp.mean(values, axis=0)).astype(jnp.bfloat16)  19.4 us
    all_to_all x2, waiting for transfers between devices, sent_to_all(): lax.all_to_all(jnp.broadcast_to(array[None], (size, *array.shape)), axis,...  17.3 us
    all_to_all x2, local copies, waits for them, and re-layouts, on_device(): lax.all_to_all(background_ensemble, 'mem', split_axis=1, concat_axis=0, t...  14.7 us
    all_to_all x1, blocking collectives, sum_at_owner(): lax.all_to_all(blocks, axis, split_axis=0, concat_axis=0, tiled=True)  13.5 us
    all_to_all x2, blocking collectives, summed_rows(): return jnp.sum(lax.all_to_all(own, far, 0, 0, tiled=True), axis=0)  11.4 us
    all_to_all x1, starting transfers between devices, sum_at_owner(): lax.all_to_all(blocks, axis, split_axis=0, concat_axis=0, tiled=True)  11.2 us
    gather x2, local copies, waits for them, and re-layouts, collect_prior(): jnp.take(realization_vectors, col_offset + local_row, axis=1)  10.4 us
  transfers between devices with their start and end apart: 4, of which 4 were waited for; matrix products, arithmetic and copies ran while one was open for 0% of the time, Pallas kernels for 0%

profile of v1, /device:TPU:1, one launch (start us, length us, event | category | flops | bytes accessed | tf_op | source)
XLA Modules:
  0.0 213.0 jit_solution(3641703116043703978)
XLA Ops:
  0.0 5.2 %copy.48 = bf16[5,2,8,32768]{3,2,0,1:T(8,128)(2,1)} copy(bf16[5,2,8,32768]{3,2,1,0:T(8,128)(2,1)} %bitcast.92) | data formatting | bytes 10485760 | tf_op jit(solution)/shard_map/all_to_all | solution.py:136
  5.2 7.5 %all-to-all-start = ((bf16[40,2,32768]{2,0,1:T(8,128)(2,1)}), bf16[40,2,32768]{2,0,1:T(8,128)(2,1)}, u32[]{:S(2)}, u32[]{:S(2)}) async-start(bf16[40,2,32768]{2,0,1:T(8,128)(2,1)} %bitcast.90), calls=%async_computation | async-start | bytes 10485760 | tf_op jit(solution)/shard_map/all_to_all | solution.py:136
  12.8 4.8 %all-to-all-done = bf16[40,2,32768]{2,0,1:T(8,128)(2,1)} async-done(((bf16[40,2,32768]{2,0,1:T(8,128)(2,1)}), bf16[40,2,32768]{2,0,1:T(8,128)(2,1)}, u32[]{:S(2)}, u32[]{:S(2)}) %all-to-all-start) | async-done | bytes 5242912 | tf_op jit(solution)/shard_map/all_to_all | solution.py:136
  17.6 9.5 %copy.32 = bf16[80,32768]{0,1:T(8,128)(2,1)} copy(bf16[80,32768]{1,0:T(8,128)(2,1)} %bitcast.9) | data formatting | bytes 10485760 | tf_op jit(solution)/shard_map/all_to_all | solution.py:136
  27.2 5.2 %gather_fusion = bf16[256,80]{1,0:T(8,128)(2,1)S(1)} fusion(bf16[80,32768]{0,1:T(8,128)(2,1)} %copy.32, s32[1024]{0:T(1024)S(1)} %pad_clamp_fusion.1), kind=kCustom, calls=%fused_computation.clone | custom fusion | bytes 82944 | tf_op jit(solution)/shard_map/jit(_take)/gather | solution.py:103
  33.4 11.2 %all-to-all-start.1 = ((f32[64,2,160]{2,1,0:T(2,128)}), f32[64,2,160]{2,1,0:T(2,128)S(1)}, u32[]{:S(2)}, u32[]{:S(2)}) async-start(f32[64,2,160]{2,1,0:T(2,128)} %copy.34), calls=%async_computation.1 | async-start | bytes 262144 | tf_op jit(solution)/shard_map/all_to_all | solution.py:23
  44.7 8.7 %all-to-all-done.1 = f32[64,2,160]{2,1,0:T(2,128)S(1)} async-done(((f32[64,2,160]{2,1,0:T(2,128)}), f32[64,2,160]{2,1,0:T(2,128)S(1)}, u32[]{:S(2)}, u32[]{:S(2)}) %all-to-all-start.1) | async-done | bytes 81952 | tf_op jit(solution)/shard_map/all_to_all | solution.py:23
  53.5 5.2 %all_to_all.74 = f32[2,1,160]{2,1,0:T(1,128)S(1)} all-to-all(f32[2,1,160]{2,1,0:T(1,128)S(1)} %all_to_all.54), channel_id=1, replica_groups=mesh['mem'=2,'state_0'=4,'state_1'=4,'state_2'=4] {'mem'}, dimensions={0} | all-to-all | bytes 2560 | tf_op jit(solution)/shard_map/all_to_all | solution.py:30
  58.7 3.7 %all_to_all.75 = f32[2,1,160]{2,1,0:T(1,128)S(1)} all-to-all(f32[2,1,160]{2,1,0:T(1,128)S(1)} %broadcast_in_dim.94), channel_id=1, replica_groups=mesh['mem'=2,'state_0'=4,'state_1'=4,'state_2'=4] {'mem'}, dimensions={0} | all-to-all | bytes 2560 | tf_op jit(solution)/shard_map/all_to_all | solution.py:42
  63.1 4.7 %all-to-all-start.4 = ((f32[64,2,160]{2,1,0:T(2,128)}), f32[64,2,160]{2,1,0:T(2,128)S(1)}, u32[]{:S(2)}, u32[]{:S(2)}) async-start(f32[64,2,160]{2,1,0:T(2,128)} %broadcast_in_dim.96), calls=%async_computation.4 | async-start | bytes 262144 | tf_op jit(solution)/shard_map/all_to_all | solution.py:42
  67.8 8.7 %all-to-all-done.4 = f32[64,2,160]{2,1,0:T(2,128)S(1)} async-done(((f32[64,2,160]{2,1,0:T(2,128)}), f32[64,2,160]{2,1,0:T(2,128)S(1)}, u32[]{:S(2)}, u32[]{:S(2)}) %all-to-all-start.4) | async-done | bytes 81952 | tf_op jit(solution)/shard_map/all_to_all | solution.py:42
  76.9 33.8 %while.32 = (s32[]{:T(128)}, bf16[80,32768]{1,0:T(8,128)(2,1)}, f32[1,256]{1,0:T(1,128)S(1)}, s32[]{:T(128)}, s32[1,256]{1,0:T(1,128)S(1)}, /*index=5*/s32[256]{...) while((s32[]{:T(128)}, bf16[80,32768]{1,0:T(8,128)(2,1)}, ...), condition=%wide.region_6.8_spmd, body=%wide.region_4.7_spmd.sunk | while | flops 348720640 | bytes 3467987 | solution.py:120
  76.9 1.2 convert_reduce_fusion.4
  78.2 2.9 %fusion.48 = bf16[80,32768]{1,0:T(8,128)(2,1)} fusion(bf16[80,32768]{1,0:T(8,128)(2,1)} %get-tuple-element.803, s32[]{:T(128)S(6)} %select_n.138, bf16[80,256]{1,0:T(8,128)(2,1)S(1)} %get-tuple-element.827, bf16[80,4096]{1,0:T(8,128)(2,1)S(1)} %get-tuple-element.772, bf16[80,256]{1,0:T(8,128)(2,1)S(1)} %get-tuple-element.825, ...), kind=kOutput, calls=%fused_computation.8.clone.1 | convolution fusion | flops 347996160 | bytes 2084868 | tf_op jit(solution)/shard_map/while/body/eval_jaxpr/dot_general | solution.py:96
  82.4 2.9 %fusion.48 = bf16[80,32768]{1,0:T(8,128)(2,1)} fusion(bf16[80,32768]{1,0:T(8,128)(2,1)} %get-tuple-element.803, s32[]{:T(128)S(6)} %select_n.138, bf16[80,256]{1,0:T(8,128)(2,1)S(1)} %get-tuple-element.827, bf16[80,4096]{1,0:T(8,128)(2,1)S(1)} %get-tuple-element.772, bf16[80,256]{1,0:T(8,128)(2,1)S(1)} %get-tuple-element.825, ...), kind=kOutput, calls=%fused_computation.8.clone.1 | convolution fusion | flops 347996160 | bytes 2084868 | tf_op jit(solution)/shard_map/while/body/eval_jaxpr/dot_general | solution.py:96
  86.6 2.9 %fusion.48 = bf16[80,32768]{1,0:T(8,128)(2,1)} fusion(bf16[80,32768]{1,0:T(8,128)(2,1)} %get-tuple-element.803, s32[]{:T(128)S(6)} %select_n.138, bf16[80,256]{1,0:T(8,128)(2,1)S(1)} %get-tuple-element.827, bf16[80,4096]{1,0:T(8,128)(2,1)S(1)} %get-tuple-element.772, bf16[80,256]{1,0:T(8,128)(2,1)S(1)} %get-tuple-element.825, ...), kind=kOutput, calls=%fused_computation.8.clone.1 | convolution fusion | flops 347996160 | bytes 2084868 | tf_op jit(solution)/shard_map/while/body/eval_jaxpr/dot_general | solution.py:96
  89.6 1.2 convert_reduce_fusion.4
  90.9 2.9 %fusion.48 = bf16[80,32768]{1,0:T(8,128)(2,1)} fusion(bf16[80,32768]{1,0:T(8,128)(2,1)} %get-tuple-element.803, s32[]{:T(128)S(6)} %select_n.138, bf16[80,256]{1,0:T(8,128)(2,1)S(1)} %get-tuple-element.827, bf16[80,4096]{1,0:T(8,128)(2,1)S(1)} %get-tuple-element.772, bf16[80,256]{1,0:T(8,128)(2,1)S(1)} %get-tuple-element.825, ...), kind=kOutput, calls=%fused_computation.8.clone.1 | convolution fusion | flops 347996160 | bytes 2084868 | tf_op jit(solution)/shard_map/while/body/eval_jaxpr/dot_general | solution.py:96
  95.1 2.9 %fusion.48 = bf16[80,32768]{1,0:T(8,128)(2,1)} fusion(bf16[80,32768]{1,0:T(8,128)(2,1)} %get-tuple-element.803, s32[]{:T(128)S(6)} %select_n.138, bf16[80,256]{1,0:T(8,128)(2,1)S(1)} %get-tuple-element.827, bf16[80,4096]{1,0:T(8,128)(2,1)S(1)} %get-tuple-element.772, bf16[80,256]{1,0:T(8,128)(2,1)S(1)} %get-tuple-element.825, ...), kind=kOutput, calls=%fused_computation.8.clone.1 | convolution fusion | flops 347996160 | bytes 2084868 | tf_op jit(solution)/shard_map/while/body/eval_jaxpr/dot_general | solution.py:96
  98.0 1.2 convert_reduce_fusion.4
  99.3 2.9 %fusion.48 = bf16[80,32768]{1,0:T(8,128)(2,1)} fusion(bf16[80,32768]{1,0:T(8,128)(2,1)} %get-tuple-element.803, s32[]{:T(128)S(6)} %select_n.138, bf16[80,256]{1,0:T(8,128)(2,1)S(1)} %get-tuple-element.827, bf16[80,4096]{1,0:T(8,128)(2,1)S(1)} %get-tuple-element.772, bf16[80,256]{1,0:T(8,128)(2,1)S(1)} %get-tuple-element.825, ...), kind=kOutput, calls=%fused_computation.8.clone.1 | convolution fusion | flops 347996160 | bytes 2084868 | tf_op jit(solution)/shard_map/while/body/eval_jaxpr/dot_general | solution.py:96
  102.2 1.2 convert_reduce_fusion.4
  103.5 2.9 %fusion.48 = bf16[80,32768]{1,0:T(8,128)(2,1)} fusion(bf16[80,32768]{1,0:T(8,128)(2,1)} %get-tuple-element.803, s32[]{:T(128)S(6)} %select_n.138, bf16[80,256]{1,0:T(8,128)(2,1)S(1)} %get-tuple-element.827, bf16[80,4096]{1,0:T(8,128)(2,1)S(1)} %get-tuple-element.772, bf16[80,256]{1,0:T(8,128)(2,1)S(1)} %get-tuple-element.825, ...), kind=kOutput, calls=%fused_computation.8.clone.1 | convolution fusion | flops 347996160 | bytes 2084868 | tf_op jit(solution)/shard_map/while/body/eval_jaxpr/dot_general | solution.py:96
  106.4 1.2 convert_reduce_fusion.4
  107.7 2.9 %fusion.48 = bf16[80,32768]{1,0:T(8,128)(2,1)} fusion(bf16[80,32768]{1,0:T(8,128)(2,1)} %get-tuple-element.803, s32[]{:T(128)S(6)} %select_n.138, bf16[80,256]{1,0:T(8,128)(2,1)S(1)} %get-tuple-element.827, bf16[80,4096]{1,0:T(8,128)(2,1)S(1)} %get-tuple-element.772, bf16[80,256]{1,0:T(8,128)(2,1)S(1)} %get-tuple-element.825, ...), kind=kOutput, calls=%fused_computation.8.clone.1 | convolution fusion | flops 347996160 | bytes 2084868 | tf_op jit(solution)/shard_map/while/body/eval_jaxpr/dot_general | solution.py:96
  110.6 9.5 %copy.36 = bf16[80,32768]{0,1:T(8,128)(2,1)} copy(bf16[80,32768]{1,0:T(8,128)(2,1)} %get-tuple-element.833) | data formatting | bytes 10485760 | tf_op jit(solution)/shard_map/while | solution.py:120
  120.1 5.2 %gather_fusion.1 = bf16[256,80]{1,0:T(8,128)(2,1)S(1)} fusion(bf16[80,32768]{0,1:T(8,128)(2,1)} %copy.36, s32[1024]{0:T(1024)S(1)} %pad_clamp_fusion), kind=kCustom, calls=%fused_computation.1.clone | custom fusion | bytes 82944 | tf_op jit(solution)/shard_map/jit(_take)/gather | solution.py:103
  125.8 13.5 %all_to_all.76 = f32[64,2,160]{2,1,0:T(2,128)S(1)} all-to-all(f32[64,2,160]{2,1,0:T(2,128)S(1)} %copy.38), channel_id=1, replica_groups=mesh['mem'=2,'state_0'=4,'state_1'=4,'state_2'=4] {'state_0','state_1','..., dimensions={0} | all-to-all | bytes 163840 | tf_op jit(solution)/shard_map/all_to_all | solution.py:23
  139.4 6.2 %all_to_all.77 = f32[2,1,160]{2,1,0:T(1,128)S(1)} all-to-all(f32[2,1,160]{2,1,0:T(1,128)S(1)} %all_to_all.59), channel_id=1, replica_groups=mesh['mem'=2,'state_0'=4,'state_1'=4,'state_2'=4] {'mem'}, dimensions={0} | all-to-all | bytes 2560 | tf_op jit(solution)/shard_map/all_to_all | solution.py:30
  145.7 3.7 %all_to_all.78 = f32[2,1,160]{2,1,0:T(1,128)S(1)} all-to-all(f32[2,1,160]{2,1,0:T(1,128)S(1)} %broadcast_in_dim.99), channel_id=1, replica_groups=mesh['mem'=2,'state_0'=4,'state_1'=4,'state_2'=4] {'mem'}, dimensions={0} | all-to-all | bytes 2560 | tf_op jit(solution)/shard_map/all_to_all | solution.py:42
  150.1 4.9 %all-to-all-start.8 = ((f32[64,2,160]{2,1,0:T(2,128)}), f32[64,2,160]{2,1,0:T(2,128)S(1)}, u32[]{:S(2)}, u32[]{:S(2)}) async-start(f32[64,2,160]{2,1,0:T(2,128)} %broadcast_in_dim.101), calls=%async_computation.8 | async-start | bytes 262144 | tf_op jit(solution)/shard_map/all_to_all | solution.py:42
  154.9 8.6 %all-to-all-done.8 = f32[64,2,160]{2,1,0:T(2,128)S(1)} async-done(((f32[64,2,160]{2,1,0:T(2,128)}), f32[64,2,160]{2,1,0:T(2,128)S(1)}, u32[]{:S(2)}, u32[]{:S(2)}) %all-to-all-start.8) | async-done | bytes 81952 | tf_op jit(solution)/shard_map/all_to_all | solution.py:42
  163.8 33.8 %while.33 = (s32[]{:T(128)}, bf16[80,32768]{1,0:T(8,128)(2,1)}, f32[1,256]{1,0:T(1,128)S(1)}, s32[]{:T(128)}, s32[1,256]{1,0:T(1,128)S(1)}, /*index=5*/s32[256]{...) while((s32[]{:T(128)}, bf16[80,32768]{1,0:T(8,128)(2,1)}, ...), condition=%wide.region_13.15_spmd, body=%wide.region_11.14_spmd.sunk | while | flops 348720640 | bytes 3467987 | solution.py:120
  163.8 1.2 convert_reduce_fusion.5
  165.1 2.9 %fusion.52 = bf16[80,32768]{1,0:T(8,128)(2,1)} fusion(bf16[80,32768]{1,0:T(8,128)(2,1)} %get-tuple-element.848, s32[]{:T(128)S(6)} %select_n.141, bf16[80,256]{1,0:T(8,128)(2,1)S(1)} %get-tuple-element.872, bf16[80,4096]{1,0:T(8,128)(2,1)S(1)} %get-tuple-element.785, bf16[80,256]{1,0:T(8,128)(2,1)S(1)} %get-tuple-element.870, ...), kind=kOutput, calls=%fused_computation.38.clone.1 | convolution fusion | flops 347996160 | bytes 2084868 | tf_op jit(solution)/shard_map/while/body/eval_jaxpr/dot_general | solution.py:96
  168.0 1.2 convert_reduce_fusion.5
  169.3 2.9 %fusion.52 = bf16[80,32768]{1,0:T(8,128)(2,1)} fusion(bf16[80,32768]{1,0:T(8,128)(2,1)} %get-tuple-element.848, s32[]{:T(128)S(6)} %select_n.141, bf16[80,256]{1,0:T(8,128)(2,1)S(1)} %get-tuple-element.872, bf16[80,4096]{1,0:T(8,128)(2,1)S(1)} %get-tuple-element.785, bf16[80,256]{1,0:T(8,128)(2,1)S(1)} %get-tuple-element.870, ...), kind=kOutput, calls=%fused_computation.38.clone.1 | convolution fusion | flops 347996160 | bytes 2084868 | tf_op jit(solution)/shard_map/while/body/eval_jaxpr/dot_general | solution.py:96
  172.3 1.2 convert_reduce_fusion.5
  173.6 2.9 %fusion.52 = bf16[80,32768]{1,0:T(8,128)(2,1)} fusion(bf16[80,32768]{1,0:T(8,128)(2,1)} %get-tuple-element.848, s32[]{:T(128)S(6)} %select_n.141, bf16[80,256]{1,0:T(8,128)(2,1)S(1)} %get-tuple-element.872, bf16[80,4096]{1,0:T(8,128)(2,1)S(1)} %get-tuple-element.785, bf16[80,256]{1,0:T(8,128)(2,1)S(1)} %get-tuple-element.870, ...), kind=kOutput, calls=%fused_computation.38.clone.1 | convolution fusion | flops 347996160 | bytes 2084868 | tf_op jit(solution)/shard_map/while/body/eval_jaxpr/dot_general | solution.py:96
  177.8 3.0 %fusion.52 = bf16[80,32768]{1,0:T(8,128)(2,1)} fusion(bf16[80,32768]{1,0:T(8,128)(2,1)} %get-tuple-element.848, s32[]{:T(128)S(6)} %select_n.141, bf16[80,256]{1,0:T(8,128)(2,1)S(1)} %get-tuple-element.872, bf16[80,4096]{1,0:T(8,128)(2,1)S(1)} %get-tuple-element.785, bf16[80,256]{1,0:T(8,128)(2,1)S(1)} %get-tuple-element.870, ...), kind=kOutput, calls=%fused_computation.38.clone.1 | convolution fusion | flops 347996160 | bytes 2084868 | tf_op jit(solution)/shard_map/while/body/eval_jaxpr/dot_general | solution.py:96
  180.7 1.2 convert_reduce_fusion.5
  182.0 2.9 %fusion.52 = bf16[80,32768]{1,0:T(8,128)(2,1)} fusion(bf16[80,32768]{1,0:T(8,128)(2,1)} %get-tuple-element.848, s32[]{:T(128)S(6)} %select_n.141, bf16[80,256]{1,0:T(8,128)(2,1)S(1)} %get-tuple-element.872, bf16[80,4096]{1,0:T(8,128)(2,1)S(1)} %get-tuple-element.785, bf16[80,256]{1,0:T(8,128)(2,1)S(1)} %get-tuple-element.870, ...), kind=kOutput, calls=%fused_computation.38.clone.1 | convolution fusion | flops 347996160 | bytes 2084868 | tf_op jit(solution)/shard_map/while/body/eval_jaxpr/dot_general | solution.py:96
  186.2 2.9 %fusion.52 = bf16[80,32768]{1,0:T(8,128)(2,1)} fusion(bf16[80,32768]{1,0:T(8,128)(2,1)} %get-tuple-element.848, s32[]{:T(128)S(6)} %select_n.141, bf16[80,256]{1,0:T(8,128)(2,1)S(1)} %get-tuple-element.872, bf16[80,4096]{1,0:T(8,128)(2,1)S(1)} %get-tuple-element.785, bf16[80,256]{1,0:T(8,128)(2,1)S(1)} %get-tuple-element.870, ...), kind=kOutput, calls=%fused_computation.38.clone.1 | convolution fusion | flops 347996160 | bytes 2084868 | tf_op jit(solution)/shard_map/while/body/eval_jaxpr/dot_general | solution.py:96
  190.4 2.9 %fusion.52 = bf16[80,32768]{1,0:T(8,128)(2,1)} fusion(bf16[80,32768]{1,0:T(8,128)(2,1)} %get-tuple-element.848, s32[]{:T(128)S(6)} %select_n.141, bf16[80,256]{1,0:T(8,128)(2,1)S(1)} %get-tuple-element.872, bf16[80,4096]{1,0:T(8,128)(2,1)S(1)} %get-tuple-element.785, bf16[80,256]{1,0:T(8,128)(2,1)S(1)} %get-tuple-element.870, ...), kind=kOutput, calls=%fused_computation.38.clone.1 | convolution fusion | flops 347996160 | bytes 2084868 | tf_op jit(solution)/shard_map/while/body/eval_jaxpr/dot_general | solution.py:96
  194.7 2.9 %fusion.52 = bf16[80,32768]{1,0:T(8,128)(2,1)} fusion(bf16[80,32768]{1,0:T(8,128)(2,1)} %get-tuple-element.848, s32[]{:T(128)S(6)} %select_n.141, bf16[80,256]{1,0:T(8,128)(2,1)S(1)} %get-tuple-element.872, bf16[80,4096]{1,0:T(8,128)(2,1)S(1)} %get-tuple-element.785, bf16[80,256]{1,0:T(8,128)(2,1)S(1)} %get-tuple-element.870, ...), kind=kOutput, calls=%fused_computation.38.clone.1 | convolution fusion | flops 347996160 | bytes 2084868 | tf_op jit(solution)/shard_map/while/body/eval_jaxpr/dot_general | solution.py:96
  197.6 2.9 %slice_bitcast_fusion.1 = (bf16[1,40,32768]{2,1,0:T(8,128)(2,1)S(1)}, bf16[1,40,32768]{2,1,0:T(8,128)(2,1)S(1)}) fusion(bf16[80,32768]{1,0:T(8,128)(2,1)} %get-tuple-element.545), kind=kLoop, calls=%fused_computation.65 | loop fusion | bytes 10485760 | tf_op jit(solution)/shard_map/stack | solution.py:180
  200.9 9.3 %all_to_all.79 = bf16[2,40,32768]{2,1,0:T(8,128)(2,1)S(1)} all-to-all(bf16[2,40,32768]{2,1,0:T(8,128)(2,1)S(1)} %pad_maximum_fusion), channel_id=1, replica_groups=mesh['mem'=2,'state_0'=4,'state_1'=4,'state_2'=4] {'mem'}, dimensions={0} | all-to-all | bytes 10485760 | tf_op jit(solution)/shard_map/all_to_all | solution.py:179
  210.3 2.7 %copy.44 = bf16[2,5,8,32768]{3,2,0,1:T(8,128)(2,1)} copy(bf16[2,5,8,32768]{3,2,1,0:T(8,128)(2,1)S(1)} %bitcast.91) | data formatting | bytes 10485760 | tf_op jit(solution)/shard_map/reshape | solution.py:178
  (147 shorter events, 13.6 us)
Async XLA Ops:
  5.2 7.5 %copy-start = (s32[2,256]{1,0:T(2,128)S(1)}, s32[2,256]{1,0:T(2,128)}, u32[]{:S(2)}) copy-start(s32[2,256]{1,0:T(2,128)} %param.14) | copy-start | bytes 6148
  5.2 7.5 %copy-start.4 = (s32[2,256]{1,0:T(2,128)S(1)}, s32[2,256]{1,0:T(2,128)}, u32[]{:S(2)}) copy-start(s32[2,256]{1,0:T(2,128)} %param.19) | copy-start | bytes 6148
  5.2 7.5 %copy-start.5 = (s32[2,256]{1,0:T(2,128)S(1)}, s32[2,256]{1,0:T(2,128)}, u32[]{:S(2)}) copy-start(s32[2,256]{1,0:T(2,128)} %param.15) | copy-start | bytes 6148
  5.2 12.4 %all-to-all-start = ((bf16[40,2,32768]{2,0,1:T(8,128)(2,1)}), bf16[40,2,32768]{2,0,1:T(8,128)(2,1)}, u32[]{:S(2)}, u32[]{:S(2)}) async-start(bf16[40,2,32768]{2,0,1:T(8,128)(2,1)} %bitcast.90), calls=%async_computation | async-start | bytes 10485760 | tf_op jit(solution)/shard_map/all_to_all | solution.py:136
  17.6 27.1 %copy-start.1 = (f32[2,256]{1,0:T(2,128)S(1)}, f32[2,256]{1,0:T(2,128)}, u32[]{:S(2)}) copy-start(f32[2,256]{1,0:T(2,128)} %param.18) | copy-start | bytes 6148
  17.6 59.2 %copy-start.2 = (f32[2,256]{1,0:T(2,128)S(1)}, f32[2,256]{1,0:T(2,128)}, u32[]{:S(2)}) copy-start(f32[2,256]{1,0:T(2,128)} %param.16) | copy-start | bytes 6148
  17.6 59.2 %copy-start.3 = (f32[2,256]{1,0:T(2,128)S(1)}, f32[2,256]{1,0:T(2,128)}, u32[]{:S(2)}) copy-start(f32[2,256]{1,0:T(2,128)} %param.17) | copy-start | bytes 6148
  33.4 20.0 %all-to-all-start.1 = ((f32[64,2,160]{2,1,0:T(2,128)}), f32[64,2,160]{2,1,0:T(2,128)S(1)}, u32[]{:S(2)}, u32[]{:S(2)}) async-start(f32[64,2,160]{2,1,0:T(2,128)} %copy.34), calls=%async_computation.1 | async-start | bytes 262144 | tf_op jit(solution)/shard_map/all_to_all | solution.py:23
  63.1 13.4 %all-to-all-start.4 = ((f32[64,2,160]{2,1,0:T(2,128)}), f32[64,2,160]{2,1,0:T(2,128)S(1)}, u32[]{:S(2)}, u32[]{:S(2)}) async-start(f32[64,2,160]{2,1,0:T(2,128)} %broadcast_in_dim.96), calls=%async_computation.4 | async-start | bytes 262144 | tf_op jit(solution)/shard_map/all_to_all | solution.py:42
  150.1 13.4 %all-to-all-start.8 = ((f32[64,2,160]{2,1,0:T(2,128)}), f32[64,2,160]{2,1,0:T(2,128)S(1)}, u32[]{:S(2)}, u32[]{:S(2)}) async-start(f32[64,2,160]{2,1,0:T(2,128)} %broadcast_in_dim.101), calls=%async_computation.8 | async-start | bytes 262144 | tf_op jit(solution)/shard_map/all_to_all | solution.py:42
